TPU v7x, 512 devices: a whole 4x8x8 slice. The times are simulated.
512 devices in a mesh: img: 8 (over x, core), atom: 64 (over z, y).
Axes of the slice: x: 4, y: 8, z: 8, core: 2. Of those that a mesh axis runs over, the one named last changes fastest.
Arguments:
- density: bfloat16 [8, 9, 9, 196608], P('img', None, None, 'atom'), may hold values from -1.5 to 1.5
- energy_density: bfloat16 [8, 9, 9, 196608], P('img', None, None, 'atom'), may hold values from -1.5 to 1.5
- dham: bfloat16 [8, 3, 9, 9, 196608], P('img', None, None, None, 'atom'), may hold values from -1.5 to 1.5
- dovl: bfloat16 [8, 3, 9, 9, 196608], P('img', None, None, None, 'atom'), may hold values from -1.5 to 1.5
- pair_owner: int32 [8, 196608], P('img', 'atom'), may hold values from 0 to 511
- pair_partner: int32 [8, 196608], P('img', 'atom'), may hold values from 0 to 32767, as said below
- partner_species: int32 [8, 196608], P('img', 'atom'), may hold values from 0 to 3, as said below
- pair_count: int32 [8, 64], P('img', 'atom'), may hold values from 768 to 3072, as said below
- species: int32 [32768], P('atom'), may hold values from 0 to 3
- orbitals: int32 [4], replicated, may hold values from 1 to 9, as said below
- coords: float32 [8, 3, 32768], P('img', None, 'atom')
- reactant: float32 [3, 32768], P(None, 'atom')
- product: float32 [3, 32768], P(None, 'atom')
Outputs:
- band_force: float32 [8, 3, 32768], P('img', None, 'atom')
- tangent_force: float32 [8], P('img')
Inputs may be any that keep to these rules, and one draw needn't show every extreme that they name: `pair_count`: each owner's live slots are its first ones; in every image some owner has all 3072 slots live, and every owner at least a quarter of them. partner_species[i, p] equals species[pair_partner[i, p]]. `pair_partner`: partners may be any atoms of the image; the first slot of owner o has its partner among the atoms of owner (o + 32) modulo 64 (owner o holds atoms o * 512 to o * 512 + 511). Species 0 has all 9 orbitals and the last species one.
All inputs are finite; a program needn't handle non-finite values.
Results may differ from a plain program's by a relative error of at most 0.0003.
Values sent between devices are 32-bit elements; how exact they have to be, the bound alone decides.
No kernel may reach another device: no remote copies, remote signals or barrier semaphores. Data moves between devices by JAX's collectives and lax.ppermute only.
A program may use at most 64 MiB of HBM per device.

v0:
```python
import jax
import jax.numpy as jnp
from jax import lax
from jax.sharding import PartitionSpec as P

spring_const = 1.0
tangent_eps = 1e-06


def passed_along(block, axis, distance):
    devices = range(lax.axis_size(axis))
    route = [(i - distance, i) for i in devices if i - distance in devices]
    return lax.ppermute(block, axis, route)


def local(
    density,
    energy_density,
    dham,
    dovl,
    pair_owner,
    pair_partner,
    partner_species,
    pair_count,
    species,
    orbitals,
    coords,
    reactant,
    product,
):
    n_slots = density.shape[-1]
    n_orbit = density.shape[1]
    atoms_local = species.shape[0]
    total_atoms = atoms_local * lax.axis_size("atom")
    current = coords[0]
    before = passed_along(current, "img", 1)
    after = passed_along(current, "img", -1)
    first_image = lax.axis_index("img") == 0
    final_image = lax.axis_index("img") == lax.axis_size("img") - 1
    before = jnp.where(first_image, reactant, before)
    after = jnp.where(final_image, product, after)
    tangent = after - before
    ahead_part = jnp.sum((after - current) ** 2)
    behind_part = jnp.sum((current - before) ** 2)
    length_part = jnp.sum(tangent * tangent)
    ahead, behind, length = lax.psum((ahead_part, behind_part, length_part), "atom")
    unit = tangent / jnp.sqrt(length + tangent_eps)
    slots = jnp.arange(n_slots, dtype=jnp.int32)
    live = slots < pair_count[0, 0]
    owner_local = pair_owner[0]
    own_species = jnp.take(species, owner_local, axis=0)
    kinds = jnp.arange(orbitals.shape[0], dtype=jnp.int32)
    own_orbitals = jnp.sum(
        jnp.where(kinds[:, None] == own_species[None, :], orbitals[:, None], 0), axis=0
    )
    partner_orbitals = jnp.sum(
        jnp.where(kinds[:, None] == partner_species[0][None, :], orbitals[:, None], 0), axis=0
    )
    levels = jnp.arange(n_orbit, dtype=jnp.int32)
    row_ok = (levels[:, None] < own_orbitals[None, :]) & live[None, :]
    col_ok = levels[:, None] < partner_orbitals[None, :]
    mask = (row_ok[:, None, :] & col_ok[None, :, :]).astype(jnp.bfloat16)
    masked_density = density[0] * mask
    masked_energy = energy_density[0] * mask
    term_ham = jnp.einsum(
        "abp,cabp->cp", masked_density, dham[0], preferred_element_type=jnp.float32
    )
    term_ovl = jnp.einsum(
        "abp,cabp->cp", masked_energy, dovl[0], preferred_element_type=jnp.float32
    )
    pair_force = -2.0 * (term_ham - term_ovl)
    my_index = lax.axis_index("atom")
    owner_atom = my_index * atoms_local + owner_local
    partial_value = jnp.zeros((3, total_atoms), jnp.float32)
    partial_value = partial_value.at[:, owner_atom].add(pair_force)
    partial_value = partial_value.at[:, pair_partner[0]].add(-pair_force)
    summed = lax.psum(partial_value, "atom")
    force = lax.dynamic_slice_in_dim(summed, my_index * atoms_local, atoms_local, 1)
    tangent_force = lax.psum(jnp.sum(force * unit), "atom")
    spring = spring_const * (jnp.sqrt(ahead) - jnp.sqrt(behind))
    band_force = force - tangent_force * unit + spring * unit
    return (band_force[None], jnp.reshape(tangent_force, (1,)))


def solution(mesh):
    return jax.shard_map(
        local,
        mesh=mesh,
        in_specs=(
            P("img", None, None, "atom"),
            P("img", None, None, "atom"),
            P("img", None, None, None, "atom"),
            P("img", None, None, None, "atom"),
            P("img", "atom"),
            P("img", "atom"),
            P("img", "atom"),
            P("img", "atom"),
            P("atom"),
            P(),
            P("img", None, "atom"),
            P(None, "atom"),
            P(None, "atom"),
        ),
        out_specs=(P("img", None, "atom"), P("img")),
        check_vma=False,
    )
```

profile of v0, /device:TPU:6, one launch (start us, length us, event | category | flops | bytes accessed | tf_op | source)
XLA Modules:
  0.0 412.6 jit_solution(6591623288836025931)
XLA Ops:
  7.2 0.0 copy-start
  7.2 0.0 all-reduce.3.cloned.1.call-start
  7.2 0.7 compare_select_fusion.1
  8.0 0.0 copy-done
  8.0 0.0 copy-start.3
  8.0 0.0 copy-start.6
  8.0 0.0 copy-start.9
  8.0 0.0 copy-start.2
  8.0 19.5 %gather_fusion = s32[3072]{0:T(1024)S(1)} fusion(s32[512]{0:T(512)S(1)} %copy-done, s32[3072]{0:T(1024)S(1)} %broadcast_clamp_fusion), kind=kCustom, calls=%fused_computation | custom fusion | bytes 36864 | tf_op jit(solution)/shard_map/jit(_take)/gather | solution.py:51
  27.6 0.0 copy-done.3
  28.3 0.0 copy-done.6
  28.3 0.0 copy-done.9
  28.3 0.1 select_reduce_fusion.1
  28.4 0.1 iota_compare_fusion
  28.5 0.0 copy-done.2
  28.5 0.0 copy-start.1
  28.5 1.9 fusion.7
  30.4 0.0 copy-done.1
  30.4 1.2 multiply_reduce_fusion.1
  31.6 0.5 copy.36
  32.1 0.0 copy-start.5
  32.1 2.7 multiply_reduce_fusion
  34.8 0.5 copy.44
  35.3 0.0 copy-done.5
  35.3 23.8 %scatter_custom_fusion = f32[3,32768]{0,1:T(8,128)} fusion(s32[3072]{0:T(1024)S(1)} %bitcast.50, f32[]{:T(128)} %constant.13.clone.1, f32[3072,3]{1,0:T(8,128)S(1)} %copy.36, f32[3072,3]{1,0:T(8,128)S(1)} %copy.44, f32[]{:T(128)} %constant.38.clone.1), kind=kCustom, calls=%fused_computation.3 | custom fusion | flops 27648 | bytes 3538952 | tf_op jit(solution)/shard_map/scatter-add | solution.py:75
  59.1 28.4 %scatter_custom_fusion.1 = f32[3,32768]{0,1:T(8,128)} fusion(f32[3,32768]{0,1:T(8,128)} %scatter_custom_fusion, s32[3072]{0:T(1024)S(1)} %bitcast.48, f32[3072,3]{1,0:T(8,128)S(1)} %copy.36, f32[3072,3]{1,0:T(8,128)S(1)} %copy.44, f32[]{:T(128)} %constant.38.clone.1), kind=kCustom, calls=%fused_computation.9 | custom fusion | flops 36864 | bytes 3539456 | tf_op jit(solution)/shard_map/scatter-add | solution.py:76
  87.5 0.0 copy-start.4
  87.5 0.0 copy-start.7
  87.5 0.0 copy-start.8
  87.5 9.9 %copy.27 = f32[3,32768]{1,0:T(4,128)} copy(f32[3,32768]{0,1:T(8,128)} %scatter_custom_fusion.1) | data formatting | bytes 786432 | tf_op jit(solution)/shard_map/scatter-add | solution.py:76
  97.3 0.0 all-reduce.3.cloned.1.call-update
  97.4 0.0 copy-done.4
  97.4 2.2 collective-permute-start
  99.6 2.1 collective-permute-start.1
  101.7 0.0 collective-permute-done
  101.8 2.8 collective-permute-done.1
  104.6 0.0 copy-done.7
  104.6 0.0 copy-done.8
  104.6 0.7 multiply_reduce_fusion.5
  105.3 150.7 %psum.36 = f32[]{:T(128)} all-reduce(f32[]{:T(128)} %get-tuple-element.17), channel_id=1, replica_groups=mesh['img'=8,'atom'=64] {'atom'}, use_global_device_ids=true, to_apply=%region_6.7 | all-reduce | flops 1 | bytes 8 | tf_op jit(solution)/shard_map/psum | solution.py:46
  256.6 2.9 all-reduce.3.cloned.1.call-done
  259.5 1.3 multiply_reduce_fusion.4
  260.8 141.6 %all-reduce = (f32[]{:T(128)}, f32[]{:T(128)}, f32[]{:T(128)}) all-reduce(f32[]{:T(128)} %get-tuple-element.21, f32[]{:T(128)} %get-tuple-element.22, f32[]{:T(128)} %multiply_reduce_fusion.4), channel_id=1, replica_groups=mesh['img'=8,'atom'=64] {'atom'}, use_global_device_ids=true, to_apply=%region_10.11 | all-reduce | flops 3 | bytes 24 | tf_op jit(solution)/shard_map/psum | solution.py:46
  403.7 1.4 add_bitcast_fusion
  405.1 0.6 copy.28
  (5 shorter events, 0.1 us)
Async XLA Ops:
  7.2 0.8 copy-start
  7.2 252.3 %all-reduce.3.cloned.1.call-start = ((), (), s32[]{:S(2)}) async-start(), calls=%async_computation | async-start | bytes 1048576 | tf_op jit(solution)/shard_map/psum | solution.py:77
  8.0 19.6 %copy-start.3 = (s32[1,3072]{1,0:T(1,128)S(1)}, s32[1,3072]{1,0:T(1,128)}, u32[]{:S(2)}) copy-start(s32[1,3072]{1,0:T(1,128)} %param.17) | copy-start | bytes 36868
  8.0 20.3 %copy-start.6 = (s32[1,3072]{1,0:T(1,128)S(1)}, s32[1,3072]{1,0:T(1,128)}, u32[]{:S(2)}) copy-start(s32[1,3072]{1,0:T(1,128)} %param.19) | copy-start | bytes 36868
  8.0 20.3 %copy-start.9 = (s32[4]{0:T(128)S(1)}, s32[4]{0:T(128)}, u32[]{:S(2)}) copy-start(s32[4]{0:T(128)} %param.22) | copy-start | bytes 52
  8.0 20.5 %copy-start.2 = (bf16[1,9,9,3072]{3,2,1,0:T(8,128)(2,1)S(1)}, bf16[1,9,9,3072]{3,2,1,0:T(8,128)(2,1)}, u32[]{:S(2)}) copy-start(bf16[1,9,9,3072]{3,2,1,0:T(8,128)(2,1)} %param.14) | copy-start | bytes 1492996
  28.5 1.9 copy-start.1
  32.1 3.2 copy-start.5
  87.5 9.9 %copy-start.4 = (f32[1,3,512]{2,0,1:T(1,128)S(1)}, f32[1,3,512]{2,0,1:T(1,128)}, u32[]{:S(2)}) copy-start(f32[1,3,512]{2,0,1:T(1,128)} %param.23) | copy-start | bytes 18436
  87.5 17.1 %copy-start.7 = (f32[3,512]{1,0:T(4,128)S(1)}, f32[3,512]{1,0:T(4,128)}, u32[]{:S(2)}) copy-start(f32[3,512]{1,0:T(4,128)} %param.24) | copy-start | bytes 18436
  87.5 17.1 %copy-start.8 = (f32[3,512]{1,0:T(4,128)S(1)}, f32[3,512]{1,0:T(4,128)}, u32[]{:S(2)}) copy-start(f32[3,512]{1,0:T(4,128)} %param.25) | copy-start | bytes 18436
  97.4 4.3 %collective-permute-start = (f32[3,512]{1,0:T(4,128)S(1)}, f32[3,512]{1,0:T(4,128)S(1)}, u32[]{:S(2)}, u32[]{:S(2)}) collective-permute-start(f32[3,512]{1,0:T(4,128)S(1)} %bitcast.51), channel_id=1, source_target_pairs={{64,0},{128,64},{192,128},{256,192},{320,256},{384,320},{448,384},... | collective-permute-start | bytes 18440 | tf_op jit(solution)/shard_map/ppermute | solution.py:13
  99.6 5.0 %collective-permute-start.1 = (f32[3,512]{1,0:T(4,128)S(1)}, f32[3,512]{1,0:T(4,128)S(1)}, u32[]{:S(2)}, u32[]{:S(2)}) collective-permute-start(f32[3,512]{1,0:T(4,128)S(1)} %bitcast.52), channel_id=1, source_target_pairs={{0,64},{64,128},{128,192},{192,256},{256,320},{320,384},{384,448},... | collective-permute-start | bytes 18440 | tf_op jit(solution)/shard_map/ppermute | solution.py:13
Sparse Core Ops, SparseCore 0:
  97.5 161.9 all-reduce.2
where the time goes:
time: 413 us
  blocking collectives  292 us (71%)
  other arithmetic  62.2 us (15%)
  local copies, waits for them, and re-layouts  31 us (8%)
  between operations  16.9 us (4%)
  waiting for transfers between devices  5.71 us (1%)
  starting transfers between devices  4.36 us (1%)
    psum x2, blocking collectives, local(): lax.psum((ahead_part, behind_part, length_part), 'atom')  292 us
    scatter-add x1, other arithmetic, local(): partial_value = partial_value.at[:, pair_partner[0]].add(-pair_force)  28.4 us
    scatter-add x1, other arithmetic, local(): partial_value = partial_value.at[:, owner_atom].add(pair_force)  23.8 us
    gather x1, local copies, waits for them, and re-layouts, local(): own_species = jnp.take(species, owner_local, axis=0)  19.5 us
    scatter-add x1, local copies, waits for them, and re-layouts, local(): partial_value = partial_value.at[:, pair_partner[0]].add(-pair_force)  9.86 us
  transfers between devices with their start and end apart: 3, of which 2 were waited for; matrix products, arithmetic and copies ran while one was open for 0% of the time, Pallas kernels for 0%

commit v1 on v0

v1 whole, which is shorter than its diff:
```python
import jax
import jax.numpy as jnp
from jax import lax
from jax.experimental import pallas as pl
from jax.experimental.pallas import tpu as pltpu
from jax.sharding import PartitionSpec as P

spring_const = 1.0
tangent_eps = 1e-06
LANES = 128
CHUNK = 512

VMEM = pl.BlockSpec(memory_space=pltpu.VMEM)
SMEM = pl.BlockSpec(memory_space=pltpu.SMEM)


def cost(flops, moved):
    return pl.CostEstimate(flops=flops, bytes_accessed=moved, transcendentals=0)


def passed_along(block, axis, distance):
    devices = range(lax.axis_size(axis))
    route = [(i - distance, i) for i in devices if i - distance in devices]
    return lax.ppermute(block, axis, route)


def limits_kernel(
    orbitals_ref, count_ref, species_ref, owner_ref, partner_kind_ref, own_ref, other_ref
):
    def orbitals_of(kind):
        found = jnp.zeros_like(kind)
        for k in range(orbitals_ref.shape[0]):
            found = jnp.where(kind == k, orbitals_ref[k], found)
        return found

    rows = owner_ref.shape[0]
    table = orbitals_of(species_ref[...])
    owner = owner_ref[...]
    block, lane = owner // LANES, owner % LANES
    own = jnp.zeros_like(owner)
    for q in range(table.shape[0]):
        row = jnp.broadcast_to(table[q : q + 1, :], (rows, LANES))
        own = jnp.where(block == q, jnp.take_along_axis(row, lane, axis=1), own)
    slot = lax.broadcasted_iota(jnp.int32, (rows, LANES), 0) * LANES
    slot = slot + lax.broadcasted_iota(jnp.int32, (rows, LANES), 1)
    own_ref[...] = jnp.where(slot < count_ref[0, 0], own, 0)
    other_ref[...] = orbitals_of(partner_kind_ref[...])


def two_pieces(value):
    high = value.astype(jnp.bfloat16)
    low = (value - high.astype(jnp.float32)).astype(jnp.bfloat16)
    return high, low


def product_nt(a, b):
    return lax.dot_general(
        a, b, (((1,), (1,)), ((), ())), preferred_element_type=jnp.float32
    )


def scatter_kernel(blocks, owners, force_ref, owner_ref, partner_ref, sent_ref, own_ref):
    n_slots = force_ref.shape[1]
    local = blocks * LANES
    total = jnp.zeros((blocks * owners, 3 * LANES), jnp.float32)
    own_total = jnp.zeros((2 * 3 * blocks, LANES), jnp.float32)
    for start in range(0, n_slots, CHUNK):
        span = pl.ds(start, CHUNK)
        partner = partner_ref[:, span]
        row = (partner % local) // LANES * owners + partner // local
        rows = lax.broadcasted_iota(jnp.int32, (blocks * owners, CHUNK), 0)
        choose_row = jnp.where(rows == row, 1.0, 0.0).astype(jnp.bfloat16)
        lanes = lax.broadcasted_iota(jnp.int32, (LANES, CHUNK), 0)
        at_lane = lanes == partner % LANES
        force = force_ref[:, span]
        high, low = two_pieces(force)
        high32, low32 = high.astype(jnp.float32), low.astype(jnp.float32)
        for piece in (high32, low32):
            spread = jnp.concatenate(
                [jnp.where(at_lane, piece[c : c + 1, :], 0.0) for c in range(3)], axis=0
            ).astype(jnp.bfloat16)
            total = total + product_nt(choose_row, spread)
        owner = owner_ref[:, span]
        own_lane = jnp.where(lanes == owner % LANES, 1.0, 0.0).astype(jnp.bfloat16)
        blocks_at = lax.broadcasted_iota(jnp.int32, (blocks, CHUNK), 0) == owner // LANES
        own_rows = jnp.concatenate(
            [
                jnp.where(blocks_at, piece[c : c + 1, :], 0.0)
                for piece in (high32, low32)
                for c in range(3)
            ],
            axis=0,
        ).astype(jnp.bfloat16)
        own_total = own_total + product_nt(own_rows, own_lane)
    for c in range(3):
        for q in range(blocks):
            sent_ref[pl.ds(c * blocks + q, owners, stride=3 * blocks), :] = -total[
                q * owners : (q + 1) * owners, c * LANES : (c + 1) * LANES
            ]
    own_ref[...] = own_total[: 3 * blocks, :] + own_total[3 * blocks :, :]


def force_kernel(
    blocks, owners, images,
    image_ref, got_ref, own_ref, now_ref, prior_ref, later_ref, first_ref, last_ref,
    force_ref, tangent_ref, parts_ref,
):
    is_first = image_ref[0] == 0
    is_last = image_ref[0] == images - 1
    zero = jnp.zeros((1, LANES), jnp.float32)
    ahead, behind, length, along = zero, zero, zero, zero
    for c in range(3):
        for q in range(blocks):
            k = c * blocks + q
            at = pl.ds(q * LANES, LANES)
            now = now_ref[c, :, at]
            prior = jnp.where(is_first, first_ref[c : c + 1, at], prior_ref[c, :, at])
            later = jnp.where(is_last, last_ref[c : c + 1, at], later_ref[c, :, at])
            tangent = later - prior
            got = got_ref[pl.ds(k, owners, stride=3 * blocks), :]
            force = own_ref[k : k + 1, :] + jnp.sum(got, axis=0, keepdims=True)
            ahead = ahead + (later - now) ** 2
            behind = behind + (now - prior) ** 2
            length = length + tangent * tangent
            along = along + force * tangent
            force_ref[k : k + 1, :] = force
            tangent_ref[k : k + 1, :] = tangent
    place = lax.broadcasted_iota(jnp.int32, (1, LANES), 1)
    parts = zero
    for at, part in enumerate((ahead, behind, length, along)):
        parts = jnp.where(place == at, jnp.sum(part, axis=1, keepdims=True), parts)
    parts_ref[...] = jnp.broadcast_to(parts, parts_ref.shape)


def band_kernel(blocks, parts_ref, force_ref, tangent_ref, band_ref, along_ref):
    parts = jnp.sum(parts_ref[...], axis=0, keepdims=True)
    ahead, behind, length, along = (parts[:, at : at + 1] for at in range(4))
    root = jnp.sqrt(length + tangent_eps)
    along = along / root
    spring = spring_const * (jnp.sqrt(ahead) - jnp.sqrt(behind))
    push = spring - along
    for c in range(3):
        for q in range(blocks):
            k = c * blocks + q
            unit = tangent_ref[k : k + 1, :] / root
            band_ref[c, :, pl.ds(q * LANES, LANES)] = force_ref[k : k + 1, :] + push * unit
    along_ref[...] = jnp.broadcast_to(along, along_ref.shape)


def local(
    density,
    energy_density,
    dham,
    dovl,
    pair_owner,
    pair_partner,
    partner_species,
    pair_count,
    species,
    orbitals,
    coords,
    reactant,
    product,
):
    n_slots = density.shape[-1]
    n_orbit = density.shape[1]
    atoms_local = species.shape[0]
    blocks = atoms_local // LANES
    owners = lax.axis_size("atom")
    images = lax.axis_size("img")
    rows = 3 * blocks
    f32, i32 = jnp.float32, jnp.int32

    current = jnp.transpose(coords, (1, 0, 2))
    before = passed_along(current, "img", 1)
    after = passed_along(current, "img", -1)

    own_orbitals, partner_orbitals = pl.pallas_call(
        limits_kernel,
        out_shape=[jax.ShapeDtypeStruct((n_slots // LANES, LANES), i32)] * 2,
        in_specs=[SMEM, SMEM, VMEM, VMEM, VMEM],
        out_specs=[VMEM, VMEM],
        compiler_params=pltpu.CompilerParams(vmem_limit_bytes=16 << 20),
        cost_estimate=cost(10 * n_slots, 16 * n_slots),
        name="limits",
    )(
        orbitals,
        pair_count,
        species.reshape(blocks, LANES),
        pair_owner.reshape(-1, LANES),
        partner_species.reshape(-1, LANES),
    )
    own_orbitals = own_orbitals.reshape(n_slots)
    partner_orbitals = partner_orbitals.reshape(n_slots)
    levels = jnp.arange(n_orbit, dtype=jnp.int32)
    row_ok = levels[:, None] < own_orbitals[None, :]
    col_ok = levels[:, None] < partner_orbitals[None, :]
    mask = (row_ok[:, None, :] & col_ok[None, :, :]).astype(jnp.bfloat16)
    masked_density = density[0] * mask
    masked_energy = energy_density[0] * mask
    term_ham = jnp.einsum(
        "abp,cabp->cp", masked_density, dham[0], preferred_element_type=jnp.float32
    )
    term_ovl = jnp.einsum(
        "abp,cabp->cp", masked_energy, dovl[0], preferred_element_type=jnp.float32
    )
    pair_force = -2.0 * (term_ham - term_ovl)

    sent, own = pl.pallas_call(
        lambda *refs: scatter_kernel(blocks, owners, *refs),
        out_shape=[
            jax.ShapeDtypeStruct((owners * rows, LANES), f32),
            jax.ShapeDtypeStruct((rows, LANES), f32),
        ],
        in_specs=[VMEM] * 3,
        out_specs=[VMEM] * 2,
        compiler_params=pltpu.CompilerParams(vmem_limit_bytes=16 << 20),
        cost_estimate=cost(4 * n_slots * owners * rows * LANES, 4 * owners * rows * LANES),
        name="scatter",
    )(pair_force, pair_owner, pair_partner)
    got = lax.all_to_all(sent.reshape(owners, rows * LANES), "atom", 0, 0, tiled=True)

    force, tangent, parts = pl.pallas_call(
        lambda *refs: force_kernel(blocks, owners, images, *refs),
        out_shape=[
            jax.ShapeDtypeStruct((rows, LANES), f32),
            jax.ShapeDtypeStruct((rows, LANES), f32),
            jax.ShapeDtypeStruct((owners, LANES), f32),
        ],
        in_specs=[SMEM] + [VMEM] * 7,
        out_specs=[VMEM] * 3,
        compiler_params=pltpu.CompilerParams(vmem_limit_bytes=16 << 20),
        cost_estimate=cost(owners * rows * LANES, 4 * owners * rows * LANES),
        name="force",
    )(
        lax.axis_index("img").astype(i32).reshape(1),
        got.reshape(owners * rows, LANES),
        own,
        current,
        before,
        after,
        reactant,
        product,
    )
    parts = lax.all_to_all(parts, "atom", 0, 0, tiled=True)
    band, along = pl.pallas_call(
        lambda *refs: band_kernel(blocks, *refs),
        out_shape=[
            jax.ShapeDtypeStruct((3, 1, atoms_local), f32),
            jax.ShapeDtypeStruct((1, LANES), f32),
        ],
        in_specs=[VMEM] * 3,
        out_specs=[VMEM] * 2,
        compiler_params=pltpu.CompilerParams(vmem_limit_bytes=16 << 20),
        cost_estimate=cost(owners * LANES, 4 * owners * LANES),
        name="band",
    )(parts, force, tangent)
    return (jnp.transpose(band, (1, 0, 2)), along[0, :1])


def solution(mesh):
    return jax.shard_map(
        local,
        mesh=mesh,
        in_specs=(
            P("img", None, None, "atom"),
            P("img", None, None, "atom"),
            P("img", None, None, None, "atom"),
            P("img", None, None, None, "atom"),
            P("img", "atom"),
            P("img", "atom"),
            P("img", "atom"),
            P("img", "atom"),
            P("atom"),
            P(),
            P("img", None, "atom"),
            P(None, "atom"),
            P(None, "atom"),
        ),
        out_specs=(P("img", None, "atom"), P("img")),
        check_vma=False,
    )
```

time: 413 us -> 64.3 us (0.16)
  blocking collectives: 292 us -> 16.3 us
  other arithmetic: 62.2 us -> 4.54 us
  local copies, waits for them, and re-layouts: 31 us -> 3.32 us
  starting transfers between devices: 4.36 us -> 22.1 us
  between operations: 16.9 us -> 1.44 us
  waiting for transfers between devices: 5.71 us -> 11.8 us
  Pallas kernels: 0 us -> 4.37 us
    psum x2 -> x0, blocking collectives: 292 us -> none  [local(): lax.psum((ahead_part, behind_part, length_part), 'atom')]
    scatter-add x2 -> x0, other arithmetic: 52.2 us -> none  [the longest x1 28.4 us: local(): partial_value = partial_value.at[:, pair_partner[0]].add(-pair_force)]
    gather x1 -> x0, local copies, waits for them, and re-layouts: 19.5 us -> none  [local(): own_species = jnp.take(species, owner_local, axis=0)]
    all_to_all x0 -> x1, starting transfers between devices: none -> 16.6 us  [local(): lax.all_to_all(sent.reshape(owners, rows * LANES), 'atom', 0, 0, tiled=True)]
    all_to_all x0 -> x1, blocking collectives: none -> 16.3 us  [local(): parts = lax.all_to_all(parts, 'atom', 0, 0, tiled=True)]
    all_to_all x0 -> x1, waiting for transfers between devices: none -> 10.4 us  [local(): lax.all_to_all(sent.reshape(owners, rows * LANES), 'atom', 0, 0, tiled=True)]
    scatter-add x1 -> x0, local copies, waits for them, and re-layouts: 9.86 us -> none  [local(): partial_value = partial_value.at[:, pair_partner[0]].add(-pair_force)]
    pallas_call x0 -> x4, Pallas kernels: none -> 4.37 us  [the longest x1 2.77 us: local(): pl.pallas_call(lambda *refs: scatter_kernel(blocks, owners, *refs), out_s...]
where the time goes in v1:
time: 64.3 us; the launch traced here: 63.9 us
  starting transfers between devices  22.1 us (34%)
  blocking collectives  16.3 us (25%)
  waiting for transfers between devices  11.8 us (18%)
  other arithmetic  4.54 us (7%)
  Pallas kernels  4.37 us (7%)
  local copies, waits for them, and re-layouts  3.32 us (5%)
  between operations  1.44 us (2%)
    all_to_all x1, starting transfers between devices, local(): lax.all_to_all(sent.reshape(owners, rows * LANES), 'atom', 0, 0, tiled=True)  16.6 us
    all_to_all x1, blocking collectives, local(): parts = lax.all_to_all(parts, 'atom', 0, 0, tiled=True)  16.3 us
    all_to_all x1, waiting for transfers between devices, local(): lax.all_to_all(sent.reshape(owners, rows * LANES), 'atom', 0, 0, tiled=True)  10.4 us
    ppermute x2, starting transfers between devices, passed_along(): return lax.ppermute(block, axis, route)  5.56 us
    unnamed x22, local copies, waits for them, and re-layouts  3.32 us
    pallas_call x1, Pallas kernels, local(): pl.pallas_call(lambda *refs: scatter_kernel(blocks, owners, *refs), out_s...  2.77 us
    dot_general x1, other arithmetic, local(): jnp.einsum('abp,cabp->cp', masked_energy, dovl[0], preferred_element_type...  2.35 us
    unnamed x1, other arithmetic  2.1 us
  transfers between devices with their start and end apart: 3, of which 2 were waited for; matrix products, arithmetic and copies ran while one was open for 0% of the time, Pallas kernels for 0%

profile of v1, /device:TPU:6, one launch (start us, length us, event | category | flops | bytes accessed | tf_op | source)
XLA Modules:
  0.0 63.9 jit_solution(8632533879955566382)
XLA Ops:
  1.3 0.0 copy-start
  1.3 0.7 %copy-done = s32[1,3072]{1,0:T(1,128)S(1)} copy-done((s32[1,3072]{1,0:T(1,128)S(1)}, s32[1,3072]{1,0:T(1,128)}, u32[]{:S(2)}) %copy-start) | copy-done | bytes 12312
  2.0 0.0 copy-start.1
  2.0 0.7 %copy-done.1 = s32[1,3072]{1,0:T(1,128)S(1)} copy-done((s32[1,3072]{1,0:T(1,128)S(1)}, s32[1,3072]{1,0:T(1,128)}, u32[]{:S(2)}) %copy-start.1) | copy-done | bytes 12312
  2.7 0.0 copy-start.6
  2.7 0.7 %copy-done.6 = s32[512]{0:T(512)S(1)} copy-done((s32[512]{0:T(512)S(1)}, s32[512]{0:T(512)}, u32[]{:S(2)}) %copy-start.6) | copy-done | bytes 2072
  3.4 0.0 copy-start.7
  3.4 0.7 %copy-done.7 = s32[4]{0:T(128)S(1)} copy-done((s32[4]{0:T(128)S(1)}, s32[4]{0:T(128)}, u32[]{:S(2)}) %copy-start.7) | copy-done | bytes 40
  4.0 0.6 limits.1
  4.7 0.0 copy-start.9
  4.8 0.0 copy-start.10
  4.8 2.1 %fusion.3 = (f32[3072,9,9]{0,2,1:T(8,128)S(1)}, f32[3072,9,9]{0,2,1:T(8,128)S(1)}) fusion(bf16[1,9,9,3072]{3,2,1,0:T(8,128)(2,1)} %param.14, pred[9,3072]{1,0:T(8,128)(4,1)S(1)} %iota_compare_fusion, pred[9,3072]{1,0:T(8,128)(4,1)S(1)} %iota_compare_fusion.1, bf16[1,9,9,3072]{3,2,1,0:T(8,128)(2,1)} %param.13), kind=kLoop, calls=%fused_computation.7 | loop fusion | flops 1244160 | bytes 3041280
  6.9 0.0 copy-done.9
  6.9 0.5 copy-done.10
  7.4 0.0 copy-start.2
  7.4 0.0 copy-start.8
  7.4 2.4 %multiply_reduce_fusion = (f32[3072,3]{0,1:T(4,128)S(1)}, f32[3072,3]{0,1:T(4,128)S(1)}) fusion(f32[3072,9,9]{0,2,1:T(8,128)S(1)} %get-tuple-element.20, bf16[1,3,9,9,3072]{4,1,3,2,0:T(4,128)(2,1)S(1)} %copy-done.9, bf16[1,3,9,9,3072]{4,1,3,2,0:T(4,128)(2,1)S(1)} %copy-done.10, f32[3072,9,9]{0,2,1:T(8,128)S(1)} %get-tuple-element.21), kind=kLoop, calls=%fused_computation | loop fusion | flops 4460544 | bytes 5050368 | tf_op jit(solution)/shard_map/abp,cabp->cp/dot_general | solution.py:204
  9.8 0.0 copy-done.2
  9.8 0.0 copy-done.8
  9.8 0.0 copy-start.5
  9.9 0.0 copy-start.3
  9.9 0.0 copy-start.4
  9.9 2.8 %scatter.1 = (f32[768,128]{1,0:T(8,128)}, f32[12,128]{1,0:T(8,128)S(1)}) custom-call(f32[3,3072]{1,0:T(4,128)S(1)} %multiply_bitcast_fusion.refs_0_, s32[1,3072]{1,0:T(1,128)S(1)} %copy-done.2, s32[1,3072]{1,0:T(1,128)S(1)} %copy-done.8), custom_call_target="tpu_custom_call" | custom-call | flops 1207959552 | bytes 393216 | tf_op jit(solution)/shard_map/scatter/pallas_call | solution.py:209
  12.7 16.6 %all-to-all-start = ((f32[64,1,1536]{2,1,0:T(1,128)}), f32[64,1,1536]{2,1,0:T(1,128)S(1)}, u32[]{:S(2)}, u32[]{:S(2)}) async-start(f32[64,1,1536]{2,1,0:T(1,128)} %bitcast.17), calls=%async_computation | async-start | bytes 786432 | tf_op jit(solution)/shard_map/all_to_all | solution.py:221
  29.2 0.0 copy-done.5
  29.3 1.9 %collective-permute-start = (f32[3,1,512]{2,1,0:T(1,128)S(1)}, f32[3,1,512]{2,1,0:T(1,128)S(1)}, u32[]{:S(2)}, u32[]{:S(2)}) collective-permute-start(f32[3,1,512]{2,1,0:T(1,128)S(1)} %bitcast.45), channel_id=1, source_target_pairs={{0,64},{64,128},{128,192},{192,256},{256,320},{320,384},{384,448},... | collective-permute-start | bytes 18440 | tf_op jit(solution)/shard_map/ppermute | solution.py:24
  31.2 3.6 %collective-permute-start.1 = (f32[3,1,512]{2,1,0:T(1,128)S(1)}, f32[3,1,512]{2,1,0:T(1,128)S(1)}, u32[]{:S(2)}, u32[]{:S(2)}) collective-permute-start(f32[3,1,512]{2,1,0:T(1,128)S(1)} %bitcast.46), channel_id=1, source_target_pairs={{64,0},{128,64},{192,128},{256,192},{320,256},{384,320},{448,384},... | collective-permute-start | bytes 18440 | tf_op jit(solution)/shard_map/ppermute | solution.py:24
  34.8 0.0 collective-permute-done.refs_4_
  34.8 1.3 %collective-permute-done.1.refs_5_ = f32[3,1,512]{2,1,0:T(1,128)S(1)} collective-permute-done((f32[3,1,512]{2,1,0:T(1,128)S(1)}, f32[3,1,512]{2,1,0:T(1,128)S(1)}, u32[]{:S(2)}, u32[]{:S(2)}) %collective-permute-start.1) | collective-permute-done | bytes 6176 | tf_op jit(solution)/shard_map/ppermute | solution.py:24
  36.2 10.4 %all-to-all-done = f32[64,1,1536]{2,1,0:T(1,128)S(1)} async-done(((f32[64,1,1536]{2,1,0:T(1,128)}), f32[64,1,1536]{2,1,0:T(1,128)S(1)}, u32[]{:S(2)}, u32[]{:S(2)}) %all-to-all-start) | async-done | bytes 393248 | tf_op jit(solution)/shard_map/all_to_all | solution.py:221
  46.6 0.0 copy-done.3
  46.6 0.0 copy-done.4
  46.6 0.1 force.1
  46.7 16.3 %all_to_all.20 = f32[64,1,128]{2,1,0:T(1,128)S(1)} all-to-all(f32[64,1,128]{2,1,0:T(1,128)S(1)} %bitcast.40), channel_id=1, replica_groups=mesh['img'=8,'atom'=64] {'atom'}, dimensions={0} | all-to-all | bytes 65536 | tf_op jit(solution)/shard_map/all_to_all | solution.py:245
  63.1 0.8 %band.1 = (f32[3,1,512]{2,1,0:T(1,128)}, f32[1,128]{1,0:T(1,128)}) custom-call(f32[64,128]{1,0:T(8,128)S(1)} %bitcast.39, f32[12,128]{1,0:T(8,128)S(1)} %get-tuple-element.16.refs_1_, f32[12,128]{1,0:T(8,128)S(1)} %get-tuple-element.17.refs_2_), custom_call_target="tpu_custom_call" | custom-call | flops 8192 | bytes 32768 | tf_op jit(solution)/shard_map/band/pallas_call | solution.py:246
  (3 shorter events, 0.1 us)
Async XLA Ops:
  1.3 0.7 %copy-start = (s32[1,3072]{1,0:T(1,128)S(1)}, s32[1,3072]{1,0:T(1,128)}, u32[]{:S(2)}) copy-start(s32[1,3072]{1,0:T(1,128)} %param.19) | copy-start | bytes 36868
  2.0 0.7 %copy-start.1 = (s32[1,3072]{1,0:T(1,128)S(1)}, s32[1,3072]{1,0:T(1,128)}, u32[]{:S(2)}) copy-start(s32[1,3072]{1,0:T(1,128)} %refs_1_.1) | copy-start | bytes 36868
  2.7 0.7 %copy-start.6 = (s32[512]{0:T(512)S(1)}, s32[512]{0:T(512)}, u32[]{:S(2)}) copy-start(s32[512]{0:T(512)} %param.21) | copy-start | bytes 6148
  3.4 0.7 %copy-start.7 = (s32[4]{0:T(128)S(1)}, s32[4]{0:T(128)}, u32[]{:S(2)}) copy-start(s32[4]{0:T(128)} %orbitals_ref.1) | copy-start | bytes 52
  4.7 2.1 %copy-start.9 = (bf16[1,3,9,9,3072]{4,1,3,2,0:T(4,128)(2,1)S(1)}, bf16[1,3,9,9,3072]{4,1,3,2,0:T(4,128)(2,1)}, u32[]{:S(2)}) copy-start(bf16[1,3,9,9,3072]{4,1,3,2,0:T(4,128)(2,1)} %param.16) | copy-start | bytes 4478980
  4.8 2.7 %copy-start.10 = (bf16[1,3,9,9,3072]{4,1,3,2,0:T(4,128)(2,1)S(1)}, bf16[1,3,9,9,3072]{4,1,3,2,0:T(4,128)(2,1)}, u32[]{:S(2)}) copy-start(bf16[1,3,9,9,3072]{4,1,3,2,0:T(4,128)(2,1)} %param.15) | copy-start | bytes 4478980
  7.4 2.4 %copy-start.2 = (s32[1,3072]{1,0:T(1,128)S(1)}, s32[1,3072]{1,0:T(1,128)}, u32[]{:S(2)}) copy-start(s32[1,3072]{1,0:T(1,128)} %refs_1_.1) | copy-start | bytes 36868
  7.4 2.4 %copy-start.8 = (s32[1,3072]{1,0:T(1,128)S(1)}, s32[1,3072]{1,0:T(1,128)}, u32[]{:S(2)}) copy-start(s32[1,3072]{1,0:T(1,128)} %refs_2_.1) | copy-start | bytes 36868
  9.8 19.4 %copy-start.5 = (f32[1,3,512]{2,0,1:T(1,128)S(1)}, f32[1,3,512]{2,0,1:T(1,128)}, u32[]{:S(2)}) copy-start(f32[1,3,512]{2,0,1:T(1,128)} %param.23) | copy-start | bytes 18436
  9.9 36.7 %copy-start.3 = (f32[3,512]{1,0:T(4,128)S(1)}, f32[3,512]{1,0:T(4,128)}, u32[]{:S(2)}) copy-start(f32[3,512]{1,0:T(4,128)} %refs_6_.1) | copy-start | bytes 18436
  9.9 36.7 %copy-start.4 = (f32[3,512]{1,0:T(4,128)S(1)}, f32[3,512]{1,0:T(4,128)}, u32[]{:S(2)}) copy-start(f32[3,512]{1,0:T(4,128)} %refs_7_.1) | copy-start | bytes 18436
  12.7 34.0 %all-to-all-start = ((f32[64,1,1536]{2,1,0:T(1,128)}), f32[64,1,1536]{2,1,0:T(1,128)S(1)}, u32[]{:S(2)}, u32[]{:S(2)}) async-start(f32[64,1,1536]{2,1,0:T(1,128)} %bitcast.17), calls=%async_computation | async-start | bytes 786432 | tf_op jit(solution)/shard_map/all_to_all | solution.py:221
  29.3 5.6 %collective-permute-start = (f32[3,1,512]{2,1,0:T(1,128)S(1)}, f32[3,1,512]{2,1,0:T(1,128)S(1)}, u32[]{:S(2)}, u32[]{:S(2)}) collective-permute-start(f32[3,1,512]{2,1,0:T(1,128)S(1)} %bitcast.45), channel_id=1, source_target_pairs={{0,64},{64,128},{128,192},{192,256},{256,320},{320,384},{384,448},... | collective-permute-start | bytes 18440 | tf_op jit(solution)/shard_map/ppermute | solution.py:24
  31.2 5.0 %collective-permute-start.1 = (f32[3,1,512]{2,1,0:T(1,128)S(1)}, f32[3,1,512]{2,1,0:T(1,128)S(1)}, u32[]{:S(2)}, u32[]{:S(2)}) collective-permute-start(f32[3,1,512]{2,1,0:T(1,128)S(1)} %bitcast.46), channel_id=1, source_target_pairs={{64,0},{128,64},{192,128},{256,192},{320,256},{384,320},{448,384},... | collective-permute-start | bytes 18440 | tf_op jit(solution)/shard_map/ppermute | solution.py:24

commit v2 on v1

v2 whole, which is shorter than its diff:
```python
import jax
import jax.numpy as jnp
from jax import lax
from jax.experimental import pallas as pl
from jax.experimental.pallas import tpu as pltpu
from jax.sharding import PartitionSpec as P

spring_const = 1.0
tangent_eps = 1e-06
LANES = 128
CHUNK = 512
DEPTH = 2

VMEM = pl.BlockSpec(memory_space=pltpu.VMEM)
SMEM = pl.BlockSpec(memory_space=pltpu.SMEM)
HBM = pl.BlockSpec(memory_space=pltpu.HBM)


def cost(flops, moved):
    return pl.CostEstimate(flops=flops, bytes_accessed=moved, transcendentals=0)


def passed_along(block, axis, distance):
    devices = range(lax.axis_size(axis))
    route = [(i - distance, i) for i in devices if i - distance in devices]
    return lax.ppermute(block, axis, route)


def product_nt(a, b):
    return lax.dot_general(
        a, b, (((1,), (1,)), ((), ())), preferred_element_type=jnp.float32
    )


def pairs_kernel(
    blocks, owners,
    count_ref, orbitals_hbm, species_hbm, owner_hbm, partner_hbm, kind_hbm,
    density_hbm, energy_hbm, dham_hbm, dovl_hbm,
    sent_ref,
    orbitals_ref, species_ref, owner_ref, partner_ref, kind_ref,
    density_ref, energy_ref, dham_ref, dovl_ref,
    force_ref, weight_ref, energy_weight_ref, row_ref, lane_ref, own_lane_ref,
    total_ref, own_total_ref, small_sem, block_sem,
):
    f32, bf16, i32 = jnp.float32, jnp.bfloat16, jnp.int32
    n_orbit, _, n_slots = density_ref.shape
    steps = n_slots // CHUNK
    small = [
        pltpu.make_async_copy(source, target, small_sem.at[i])
        for i, (source, target) in enumerate(
            (
                (orbitals_hbm, orbitals_ref),
                (species_hbm, species_ref),
                (owner_hbm, owner_ref),
                (partner_hbm, partner_ref),
                (kind_hbm, kind_ref),
            )
        )
    ]
    for copy in small:
        copy.start()
    spans = [pl.ds(step * CHUNK, CHUNK) for step in range(steps)]
    streams = []
    for step, at in enumerate(spans):
        pieces = (
            (density_hbm.at[0, :, :, at], density_ref.at[:, :, at]),
            (energy_hbm.at[0, :, :, at], energy_ref.at[:, :, at]),
            (dham_hbm.at[0, :, :, :, at], dham_ref.at[:, :, :, at]),
            (dovl_hbm.at[0, :, :, :, at], dovl_ref.at[:, :, :, at]),
        )
        streams.append(
            [
                pltpu.make_async_copy(source, target, block_sem.at[i, step])
                for i, (source, target) in enumerate(pieces)
            ]
        )
    for step in range(DEPTH):
        for copy in streams[step]:
            copy.start()
    for copy in small:
        copy.wait()

    def orbitals_of(kind):
        found = jnp.zeros_like(kind)
        for k in range(orbitals_ref.shape[0]):
            found = jnp.where(kind == k, orbitals_ref[k], found)
        return found

    table = orbitals_of(species_ref[...]).astype(f32)
    table = jnp.concatenate([table, jnp.zeros((8 - blocks, LANES), f32)], axis=0).astype(bf16)
    local = blocks * LANES
    limits = []
    for step, at in enumerate(spans):
        owner, partner = owner_ref[:, at], partner_ref[:, at]
        lanes = lax.broadcasted_iota(i32, (LANES, CHUNK), 0)
        own_lane = jnp.where(lanes == owner % LANES, 1.0, 0.0).astype(bf16)
        own_lane_ref[:, at] = own_lane
        lane_ref[:, at] = jnp.where(lanes == partner % LANES, 1.0, 0.0).astype(bf16)
        row = (partner % local) // LANES * owners + partner // local
        rows = lax.broadcasted_iota(i32, (blocks * owners, CHUNK), 0)
        row_ref[:, at] = jnp.where(rows == row, 1.0, 0.0).astype(bf16)
        look = lax.dot_general(
            table, own_lane, (((1,), (0,)), ((), ())), preferred_element_type=f32
        )
        at_block = lax.broadcasted_iota(i32, (8, CHUNK), 0) == owner // LANES
        own = jnp.sum(jnp.where(at_block, look, 0.0), axis=0, keepdims=True).astype(i32)
        slot = step * CHUNK + lax.broadcasted_iota(i32, (1, CHUNK), 1)
        own = jnp.where(slot < count_ref[0, 0], own, 0)
        limits.append((own, orbitals_of(kind_ref[:, at])))

    def products(step):
        at = spans[step]
        own, other = limits[step]
        levels = lax.broadcasted_iota(i32, (n_orbit, CHUNK), 0)
        ham = jnp.zeros((3, CHUNK), f32)
        ovl = ham
        for a in range(n_orbit):
            keep = levels < jnp.where(own > a, other, 0)
            weight_ref[a] = jnp.where(keep, density_ref[a, :, at].astype(f32), 0.0)
            energy_weight_ref[a] = jnp.where(keep, energy_ref[a, :, at].astype(f32), 0.0)
            for b in range(n_orbit):
                ham = ham + weight_ref[a, b : b + 1, :] * dham_ref[a, b, :, at].astype(f32)
                ovl = ovl + energy_weight_ref[a, b : b + 1, :] * dovl_ref[a, b, :, at].astype(f32)
        force_ref[:, at] = -2.0 * (ham - ovl)

    def scatter(step):
        at = spans[step]
        force = force_ref[:, at]
        high = force.astype(bf16).astype(f32)
        low = (force - high).astype(bf16).astype(f32)
        hot = lane_ref[:, at]
        spread = jnp.concatenate(
            [
                hot * jnp.broadcast_to(piece[c : c + 1, :], (LANES, CHUNK)).astype(bf16)
                for piece in (high, low)
                for c in range(3)
            ],
            axis=0,
        )
        new = product_nt(row_ref[:, at], spread)
        new = new[:, : 3 * LANES] + new[:, 3 * LANES :]
        blocks_at = lax.broadcasted_iota(i32, (blocks, CHUNK), 0) == owner_ref[:, at] // LANES
        own_rows = jnp.concatenate(
            [
                jnp.where(blocks_at, piece[c : c + 1, :], 0.0)
                for piece in (high, low)
                for c in range(3)
            ],
            axis=0,
        ).astype(bf16)
        own_new = product_nt(own_rows, own_lane_ref[:, at])
        if step == 0:
            total_ref[...] = new
            own_total_ref[...] = own_new
        else:
            total_ref[...] += new
            own_total_ref[...] += own_new

    for step in range(steps):
        for copy in streams[step]:
            copy.wait()
        if step + DEPTH < steps:
            for copy in streams[step + DEPTH]:
                copy.start()
        products(step)
        if step > 0:
            scatter(step - 1)
    scatter(steps - 1)
    for c in range(3):
        for q in range(blocks):
            sent_ref[pl.ds(c * blocks + q, owners, stride=3 * blocks), :] = -total_ref[
                q * owners : (q + 1) * owners, c * LANES : (c + 1) * LANES
            ]
    mine = lax.axis_index("atom") * (3 * blocks)
    for k in range(3 * blocks):
        at = pl.ds(mine + k, 1)
        own = own_total_ref[k : k + 1, :] + own_total_ref[3 * blocks + k : 3 * blocks + k + 1, :]
        sent_ref[at, :] = sent_ref[at, :] + own


def force_kernel(
    blocks, owners, images,
    image_ref, got_ref, now_ref, prior_ref, later_ref, first_ref, last_ref,
    force_ref, tangent_ref, parts_ref,
):
    is_first = image_ref[0] == 0
    is_last = image_ref[0] == images - 1
    zero = jnp.zeros((1, LANES), jnp.float32)
    ahead, behind, length, along = zero, zero, zero, zero
    for c in range(3):
        for q in range(blocks):
            k = c * blocks + q
            at = pl.ds(q * LANES, LANES)
            now = now_ref[c, :, at]
            prior = jnp.where(is_first, first_ref[c : c + 1, at], prior_ref[c, :, at])
            later = jnp.where(is_last, last_ref[c : c + 1, at], later_ref[c, :, at])
            tangent = later - prior
            got = got_ref[pl.ds(k, owners, stride=3 * blocks), :]
            force = jnp.sum(got, axis=0, keepdims=True)
            ahead = ahead + (later - now) ** 2
            behind = behind + (now - prior) ** 2
            length = length + tangent * tangent
            along = along + force * tangent
            force_ref[k : k + 1, :] = force
            tangent_ref[k : k + 1, :] = tangent
    place = lax.broadcasted_iota(jnp.int32, (1, LANES), 1)
    parts = zero
    for at, part in enumerate((ahead, behind, length, along)):
        parts = jnp.where(place == at, jnp.sum(part, axis=1, keepdims=True), parts)
    parts_ref[...] = jnp.broadcast_to(parts, parts_ref.shape)


def band_kernel(blocks, parts_ref, force_ref, tangent_ref, band_ref, along_ref):
    parts = jnp.sum(parts_ref[...], axis=0, keepdims=True)
    ahead, behind, length, along = (parts[:, at : at + 1] for at in range(4))
    root = jnp.sqrt(length + tangent_eps)
    along = along / root
    spring = spring_const * (jnp.sqrt(ahead) - jnp.sqrt(behind))
    push = spring - along
    for c in range(3):
        for q in range(blocks):
            k = c * blocks + q
            unit = tangent_ref[k : k + 1, :] / root
            band_ref[c, :, pl.ds(q * LANES, LANES)] = force_ref[k : k + 1, :] + push * unit
    along_ref[...] = jnp.broadcast_to(along, along_ref.shape)


def local(
    density,
    energy_density,
    dham,
    dovl,
    pair_owner,
    pair_partner,
    partner_species,
    pair_count,
    species,
    orbitals,
    coords,
    reactant,
    product,
):
    n_slots = density.shape[-1]
    n_orbit = density.shape[1]
    atoms_local = species.shape[0]
    blocks = atoms_local // LANES
    owners = lax.axis_size("atom")
    images = lax.axis_size("img")
    rows = 3 * blocks
    f32, i32 = jnp.float32, jnp.int32

    current = jnp.transpose(coords, (1, 0, 2))
    before = passed_along(current, "img", 1)
    after = passed_along(current, "img", -1)

    vmem, dma = pltpu.VMEM, pltpu.SemaphoreType.DMA
    bf16 = jnp.bfloat16
    sent = pl.pallas_call(
        lambda *refs: pairs_kernel(blocks, owners, *refs),
        out_shape=jax.ShapeDtypeStruct((owners * rows, LANES), f32),
        in_specs=[SMEM] + [HBM] * 9,
        out_specs=VMEM,
        scratch_shapes=[
            pltpu.SMEM(orbitals.shape, i32),
            vmem((blocks, LANES), i32),
            vmem((1, n_slots), i32),
            vmem((1, n_slots), i32),
            vmem((1, n_slots), i32),
            vmem((n_orbit, n_orbit, n_slots), bf16),
            vmem((n_orbit, n_orbit, n_slots), bf16),
            vmem((n_orbit, n_orbit, 3, n_slots), bf16),
            vmem((n_orbit, n_orbit, 3, n_slots), bf16),
            vmem((3, n_slots), f32),
            vmem((n_orbit, n_orbit, CHUNK), f32),
            vmem((n_orbit, n_orbit, CHUNK), f32),
            vmem((blocks * owners, n_slots), bf16),
            vmem((LANES, n_slots), bf16),
            vmem((LANES, n_slots), bf16),
            vmem((blocks * owners, 3 * LANES), f32),
            vmem((2 * rows, LANES), f32),
            dma((5,)),
            dma((4, n_slots // CHUNK)),
        ],
        compiler_params=pltpu.CompilerParams(vmem_limit_bytes=63 << 20),
        cost_estimate=cost(4 * n_slots * owners * rows * LANES, 8 * 243 * n_slots),
        name="pairs",
    )(
        pair_count,
        orbitals,
        species.reshape(blocks, LANES),
        pair_owner,
        pair_partner,
        partner_species,
        density,
        energy_density,
        jnp.transpose(dham, (0, 2, 3, 1, 4)),
        jnp.transpose(dovl, (0, 2, 3, 1, 4)),
    )
    got = lax.all_to_all(sent.reshape(owners, rows * LANES), "atom", 0, 0, tiled=True)

    force, tangent, parts = pl.pallas_call(
        lambda *refs: force_kernel(blocks, owners, images, *refs),
        out_shape=[
            jax.ShapeDtypeStruct((rows, LANES), f32),
            jax.ShapeDtypeStruct((rows, LANES), f32),
            jax.ShapeDtypeStruct((owners, LANES), f32),
        ],
        in_specs=[SMEM] + [VMEM] * 6,
        out_specs=[VMEM] * 3,
        compiler_params=pltpu.CompilerParams(vmem_limit_bytes=16 << 20),
        cost_estimate=cost(owners * rows * LANES, 4 * owners * rows * LANES),
        name="force",
    )(
        lax.axis_index("img").astype(i32).reshape(1),
        got.reshape(owners * rows, LANES),
        current,
        before,
        after,
        reactant,
        product,
    )
    parts = lax.all_to_all(parts, "atom", 0, 0, tiled=True)
    band, along = pl.pallas_call(
        lambda *refs: band_kernel(blocks, *refs),
        out_shape=[
            jax.ShapeDtypeStruct((3, 1, atoms_local), f32),
            jax.ShapeDtypeStruct((1, LANES), f32),
        ],
        in_specs=[VMEM] * 3,
        out_specs=[VMEM] * 2,
        compiler_params=pltpu.CompilerParams(vmem_limit_bytes=16 << 20),
        cost_estimate=cost(owners * LANES, 4 * owners * LANES),
        name="band",
    )(parts, force, tangent)
    return (jnp.transpose(band, (1, 0, 2)), along[0, :1])


def solution(mesh):
    return jax.shard_map(
        local,
        mesh=mesh,
        in_specs=(
            P("img", None, None, "atom"),
            P("img", None, None, "atom"),
            P("img", None, None, None, "atom"),
            P("img", None, None, None, "atom"),
            P("img", "atom"),
            P("img", "atom"),
            P("img", "atom"),
            P("img", "atom"),
            P("atom"),
            P(),
            P("img", None, "atom"),
            P(None, "atom"),
            P(None, "atom"),
        ),
        out_specs=(P("img", None, "atom"), P("img")),
        check_vma=False,
    )
```

time: 64.3 us -> 60.7 us (0.944)
  other arithmetic: 4.54 us -> 0 us
  Pallas kernels: 4.37 us -> 8.78 us
  local copies, waits for them, and re-layouts: 3.32 us -> 0.01 us
    pallas_call x2 -> x1, Pallas kernels: 3.4 us -> 7.81 us  [local(): pl.pallas_call(lambda *refs: pairs_kernel(blocks, owners, *refs), out_sha...]
    unnamed x22 -> x6, local copies, waits for them, and re-layouts: 3.32 us -> 0.01 us
    dot_general x1 -> x0, other arithmetic: 2.35 us -> none  [local(): jnp.einsum('abp,cabp->cp', masked_energy, dovl[0], preferred_element_type...]
    unnamed x1 -> x0, other arithmetic: 2.1 us -> none
where the time goes in v2:
time: 60.7 us; the launch traced here: 60.4 us
  starting transfers between devices  22.2 us (37%)
  blocking collectives  16.3 us (27%)
  waiting for transfers between devices  11.8 us (19%)
  Pallas kernels  8.78 us (14%)
  between operations  1.36 us (2%)
    all_to_all x1, starting transfers between devices, local(): lax.all_to_all(sent.reshape(owners, rows * LANES), 'atom', 0, 0, tiled=True)  16.6 us
    all_to_all x1, blocking collectives, local(): parts = lax.all_to_all(parts, 'atom', 0, 0, tiled=True)  16.3 us
    all_to_all x1, waiting for transfers between devices, local(): lax.all_to_all(sent.reshape(owners, rows * LANES), 'atom', 0, 0, tiled=True)  10.4 us
    pallas_call x1, Pallas kernels, local(): pl.pallas_call(lambda *refs: pairs_kernel(blocks, owners, *refs), out_sha...  7.81 us
    ppermute x2, starting transfers between devices, passed_along(): return lax.ppermute(block, axis, route)  5.56 us
    ppermute x2, waiting for transfers between devices, passed_along(): return lax.ppermute(block, axis, route)  1.31 us
  transfers between devices with their start and end apart: 3, of which 2 were waited for; matrix products, arithmetic and copies ran while one was open for 0% of the time, Pallas kernels for 0%

profile of v2, /device:TPU:6, one launch (start us, length us, event | category | flops | bytes accessed | tf_op | source)
XLA Modules:
  0.0 60.4 jit_solution(2507495554514640583)
XLA Ops:
  1.3 0.0 copy-start.2
  1.3 0.0 copy-start
  1.3 0.0 copy-start.1
  1.3 7.8 %pairs.1 = f32[768,128]{1,0:T(8,128)} custom-call(s32[1,1]{1,0:T(1,128)S(6)} %copy.17.refs_0_, s32[4]{0:T(128)} %refs_1_.1, s32[4,128]{1,0:T(4,128)} %bitcast.23, s32[1,3072]{1,0:T(1,128)} %refs_3_.1, s32[1,3072]{1,0:T(1,128)} %refs_4_.1, s32[1,3072]{1,0:T(1,128)} %refs_5_.2, bf16[1,9,9,3072]{3,2,1,0:T(8,128)(2,1)} %refs_6_.2, ...), custom_call_target="tpu_custom_call" | custom-call | flops 1207959552 | bytes 5971968 | tf_op jit(solution)/shard_map/pairs/pallas_call | solution.py:258
  9.1 16.6 %all-to-all-start = ((f32[64,1,1536]{2,1,0:T(1,128)}), f32[64,1,1536]{2,1,0:T(1,128)S(1)}, u32[]{:S(2)}, u32[]{:S(2)}) async-start(f32[64,1,1536]{2,1,0:T(1,128)} %bitcast.22), calls=%async_computation | async-start | bytes 786432 | tf_op jit(solution)/shard_map/all_to_all | solution.py:299
  25.7 0.0 copy-done.2
  25.7 1.9 %collective-permute-start = (f32[3,1,512]{2,1,0:T(1,128)S(1)}, f32[3,1,512]{2,1,0:T(1,128)S(1)}, u32[]{:S(2)}, u32[]{:S(2)}) collective-permute-start(f32[3,1,512]{2,1,0:T(1,128)S(1)} %bitcast.17), channel_id=1, source_target_pairs={{0,64},{64,128},{128,192},{192,256},{256,320},{320,384},{384,448},... | collective-permute-start | bytes 18440 | tf_op jit(solution)/shard_map/ppermute | solution.py:26
  27.7 3.6 %collective-permute-start.1 = (f32[3,1,512]{2,1,0:T(1,128)S(1)}, f32[3,1,512]{2,1,0:T(1,128)S(1)}, u32[]{:S(2)}, u32[]{:S(2)}) collective-permute-start(f32[3,1,512]{2,1,0:T(1,128)S(1)} %bitcast.18), channel_id=1, source_target_pairs={{64,0},{128,64},{192,128},{256,192},{320,256},{384,320},{448,384},... | collective-permute-start | bytes 18440 | tf_op jit(solution)/shard_map/ppermute | solution.py:26
  31.3 0.0 collective-permute-done.refs_3_
  31.3 1.3 %collective-permute-done.1.refs_4_ = f32[3,1,512]{2,1,0:T(1,128)S(1)} collective-permute-done((f32[3,1,512]{2,1,0:T(1,128)S(1)}, f32[3,1,512]{2,1,0:T(1,128)S(1)}, u32[]{:S(2)}, u32[]{:S(2)}) %collective-permute-start.1) | collective-permute-done | bytes 6176 | tf_op jit(solution)/shard_map/ppermute | solution.py:26
  32.6 10.4 %all-to-all-done = f32[64,1,1536]{2,1,0:T(1,128)S(1)} async-done(((f32[64,1,1536]{2,1,0:T(1,128)}), f32[64,1,1536]{2,1,0:T(1,128)S(1)}, u32[]{:S(2)}, u32[]{:S(2)}) %all-to-all-start) | async-done | bytes 393248 | tf_op jit(solution)/shard_map/all_to_all | solution.py:299
  43.1 0.0 copy-done
  43.1 0.0 copy-done.1
  43.1 0.1 force.1
  43.2 16.3 %all_to_all.20 = f32[64,1,128]{2,1,0:T(1,128)S(1)} all-to-all(f32[64,1,128]{2,1,0:T(1,128)S(1)} %bitcast.16), channel_id=1, replica_groups=mesh['img'=8,'atom'=64] {'atom'}, dimensions={0} | all-to-all | bytes 65536 | tf_op jit(solution)/shard_map/all_to_all | solution.py:322
  59.5 0.8 %band.1 = (f32[3,1,512]{2,1,0:T(1,128)}, f32[1,128]{1,0:T(1,128)}) custom-call(f32[64,128]{1,0:T(8,128)S(1)} %bitcast.15, f32[12,128]{1,0:T(8,128)S(1)} %get-tuple-element.8.refs_1_, f32[12,128]{1,0:T(8,128)S(1)} %get-tuple-element.9.refs_2_), custom_call_target="tpu_custom_call" | custom-call | flops 8192 | bytes 32768 | tf_op jit(solution)/shard_map/band/pallas_call | solution.py:323
Async XLA Ops:
  1.3 24.5 %copy-start.2 = (f32[1,3,512]{2,0,1:T(1,128)S(1)}, f32[1,3,512]{2,0,1:T(1,128)}, u32[]{:S(2)}) copy-start(f32[1,3,512]{2,0,1:T(1,128)} %param.23) | copy-start | bytes 18436
  1.3 41.8 %copy-start = (f32[3,512]{1,0:T(4,128)S(1)}, f32[3,512]{1,0:T(4,128)}, u32[]{:S(2)}) copy-start(f32[3,512]{1,0:T(4,128)} %refs_5_.3) | copy-start | bytes 18436
  1.3 41.8 %copy-start.1 = (f32[3,512]{1,0:T(4,128)S(1)}, f32[3,512]{1,0:T(4,128)}, u32[]{:S(2)}) copy-start(f32[3,512]{1,0:T(4,128)} %refs_6_.3) | copy-start | bytes 18436
  9.1 34.0 %all-to-all-start = ((f32[64,1,1536]{2,1,0:T(1,128)}), f32[64,1,1536]{2,1,0:T(1,128)S(1)}, u32[]{:S(2)}, u32[]{:S(2)}) async-start(f32[64,1,1536]{2,1,0:T(1,128)} %bitcast.22), calls=%async_computation | async-start | bytes 786432 | tf_op jit(solution)/shard_map/all_to_all | solution.py:299
  25.7 5.6 %collective-permute-start = (f32[3,1,512]{2,1,0:T(1,128)S(1)}, f32[3,1,512]{2,1,0:T(1,128)S(1)}, u32[]{:S(2)}, u32[]{:S(2)}) collective-permute-start(f32[3,1,512]{2,1,0:T(1,128)S(1)} %bitcast.17), channel_id=1, source_target_pairs={{0,64},{64,128},{128,192},{192,256},{256,320},{320,384},{384,448},... | collective-permute-start | bytes 18440 | tf_op jit(solution)/shard_map/ppermute | solution.py:26
  27.7 5.0 %collective-permute-start.1 = (f32[3,1,512]{2,1,0:T(1,128)S(1)}, f32[3,1,512]{2,1,0:T(1,128)S(1)}, u32[]{:S(2)}, u32[]{:S(2)}) collective-permute-start(f32[3,1,512]{2,1,0:T(1,128)S(1)} %bitcast.18), channel_id=1, source_target_pairs={{64,0},{128,64},{192,128},{256,192},{320,256},{384,320},{448,384},... | collective-permute-start | bytes 18440 | tf_op jit(solution)/shard_map/ppermute | solution.py:26

commit v3 on v2

--- a/solution.py
+++ b/solution.py
@@ -40,7 +40,7 @@
     orbitals_ref, species_ref, owner_ref, partner_ref, kind_ref,
     density_ref, energy_ref, dham_ref, dovl_ref,
     force_ref, weight_ref, energy_weight_ref, row_ref, lane_ref, own_lane_ref,
-    total_ref, own_total_ref, small_sem, block_sem,
+    total_ref, own_total_ref, level_ref, small_sem, block_sem,
 ):
     f32, bf16, i32 = jnp.float32, jnp.bfloat16, jnp.int32
     n_orbit, _, n_slots = density_ref.shape
@@ -88,21 +88,27 @@
 
     table = orbitals_of(species_ref[...]).astype(f32)
     table = jnp.concatenate([table, jnp.zeros((8 - blocks, LANES), f32)], axis=0).astype(bf16)
-    local = blocks * LANES
+    lane_bits = LANES.bit_length() - 1
+    local_bits = (blocks * LANES).bit_length() - 1
+    level_ref[...] = (
+        lax.broadcasted_iota(i32, level_ref.shape, 0).astype(f32).astype(bf16)
+    )
+    one, zero = jnp.ones((), bf16), jnp.zeros((), bf16)
     limits = []
     for step, at in enumerate(spans):
         owner, partner = owner_ref[:, at], partner_ref[:, at]
-        lanes = lax.broadcasted_iota(i32, (LANES, CHUNK), 0)
-        own_lane = jnp.where(lanes == owner % LANES, 1.0, 0.0).astype(bf16)
+        lanes = level_ref[:LANES, :]
+        own_at = (owner & (LANES - 1)).astype(f32).astype(bf16)
+        own_lane = jnp.where(lanes == own_at, one, zero)
         own_lane_ref[:, at] = own_lane
-        lane_ref[:, at] = jnp.where(lanes == partner % LANES, 1.0, 0.0).astype(bf16)
-        row = (partner % local) // LANES * owners + partner // local
-        rows = lax.broadcasted_iota(i32, (blocks * owners, CHUNK), 0)
-        row_ref[:, at] = jnp.where(rows == row, 1.0, 0.0).astype(bf16)
+        partner_at = (partner & (LANES - 1)).astype(f32).astype(bf16)
+        lane_ref[:, at] = jnp.where(lanes == partner_at, -one, zero)
+        row = ((partner & (blocks * LANES - 1)) >> lane_bits) * owners + (partner >> local_bits)
+        row_ref[:, at] = jnp.where(level_ref[...] == row.astype(f32).astype(bf16), one, zero)
         look = lax.dot_general(
             table, own_lane, (((1,), (0,)), ((), ())), preferred_element_type=f32
         )
-        at_block = lax.broadcasted_iota(i32, (8, CHUNK), 0) == owner // LANES
+        at_block = lax.broadcasted_iota(i32, (8, CHUNK), 0) == owner >> lane_bits
         own = jnp.sum(jnp.where(at_block, look, 0.0), axis=0, keepdims=True).astype(i32)
         slot = step * CHUNK + lax.broadcasted_iota(i32, (1, CHUNK), 1)
         own = jnp.where(slot < count_ref[0, 0], own, 0)
@@ -139,7 +145,7 @@
         )
         new = product_nt(row_ref[:, at], spread)
         new = new[:, : 3 * LANES] + new[:, 3 * LANES :]
-        blocks_at = lax.broadcasted_iota(i32, (blocks, CHUNK), 0) == owner_ref[:, at] // LANES
+        blocks_at = lax.broadcasted_iota(i32, (blocks, CHUNK), 0) == owner_ref[:, at] >> lane_bits
         own_rows = jnp.concatenate(
             [
                 jnp.where(blocks_at, piece[c : c + 1, :], 0.0)
@@ -168,7 +174,7 @@
     scatter(steps - 1)
     for c in range(3):
         for q in range(blocks):
-            sent_ref[pl.ds(c * blocks + q, owners, stride=3 * blocks), :] = -total_ref[
+            sent_ref[pl.ds(c * blocks + q, owners, stride=3 * blocks), :] = total_ref[
                 q * owners : (q + 1) * owners, c * LANES : (c + 1) * LANES
             ]
     mine = lax.axis_index("atom") * (3 * blocks)
@@ -253,6 +259,8 @@
     before = passed_along(current, "img", 1)
     after = passed_along(current, "img", -1)
 
+    if (blocks * LANES) & (blocks * LANES - 1) or blocks * owners > 256:
+        raise ValueError("sizes")
     vmem, dma = pltpu.VMEM, pltpu.SemaphoreType.DMA
     bf16 = jnp.bfloat16
     sent = pl.pallas_call(
@@ -278,6 +286,7 @@
             vmem((LANES, n_slots), bf16),
             vmem((blocks * owners, 3 * LANES), f32),
             vmem((2 * rows, LANES), f32),
+            vmem((blocks * owners, CHUNK), bf16),
             dma((5,)),
             dma((4, n_slots // CHUNK)),
         ],

time: 60.7 us -> 60.1 us (level)
  no operation moved by 1% of the time
where the time goes in v3:
time: 60.1 us; the launch traced here: 59.8 us
  starting transfers between devices  22.2 us (37%)
  blocking collectives  16.3 us (27%)
  waiting for transfers between devices  11.8 us (20%)
  Pallas kernels  8.24 us (14%)
  between operations  1.36 us (2%)
    all_to_all x1, starting transfers between devices, local(): lax.all_to_all(sent.reshape(owners, rows * LANES), 'atom', 0, 0, tiled=True)  16.6 us
    all_to_all x1, blocking collectives, local(): parts = lax.all_to_all(parts, 'atom', 0, 0, tiled=True)  16.3 us
    all_to_all x1, waiting for transfers between devices, local(): lax.all_to_all(sent.reshape(owners, rows * LANES), 'atom', 0, 0, tiled=True)  10.4 us
    pallas_call x1, Pallas kernels, local(): pl.pallas_call(lambda *refs: pairs_kernel(blocks, owners, *refs), out_sha...  7.27 us
    ppermute x2, starting transfers between devices, passed_along(): return lax.ppermute(block, axis, route)  5.56 us
    ppermute x2, waiting for transfers between devices, passed_along(): return lax.ppermute(block, axis, route)  1.31 us
  transfers between devices with their start and end apart: 3, of which 2 were waited for; matrix products, arithmetic and copies ran while one was open for 0% of the time, Pallas kernels for 0%

profile of v3, /device:TPU:6, one launch (start us, length us, event | category | flops | bytes accessed | tf_op | source)
XLA Modules:
  0.0 59.8 jit_solution(7075407703699884253)
XLA Ops:
  1.3 0.0 copy-start.2
  1.3 0.0 copy-start
  1.3 0.0 copy-start.1
  1.3 7.3 %pairs.1 = f32[768,128]{1,0:T(8,128)} custom-call(s32[1,1]{1,0:T(1,128)S(6)} %copy.17.refs_0_, s32[4]{0:T(128)} %refs_1_.1, s32[4,128]{1,0:T(4,128)} %bitcast.23, s32[1,3072]{1,0:T(1,128)} %refs_3_.1, s32[1,3072]{1,0:T(1,128)} %refs_4_.1, s32[1,3072]{1,0:T(1,128)} %refs_5_.2, bf16[1,9,9,3072]{3,2,1,0:T(8,128)(2,1)} %refs_6_.2, ...), custom_call_target="tpu_custom_call" | custom-call | flops 1207959552 | bytes 5971968 | tf_op jit(solution)/shard_map/pairs/pallas_call | solution.py:266
  8.6 16.6 %all-to-all-start = ((f32[64,1,1536]{2,1,0:T(1,128)}), f32[64,1,1536]{2,1,0:T(1,128)S(1)}, u32[]{:S(2)}, u32[]{:S(2)}) async-start(f32[64,1,1536]{2,1,0:T(1,128)} %bitcast.22), calls=%async_computation | async-start | bytes 786432 | tf_op jit(solution)/shard_map/all_to_all | solution.py:308
  25.2 0.0 copy-done.2
  25.2 1.9 %collective-permute-start = (f32[3,1,512]{2,1,0:T(1,128)S(1)}, f32[3,1,512]{2,1,0:T(1,128)S(1)}, u32[]{:S(2)}, u32[]{:S(2)}) collective-permute-start(f32[3,1,512]{2,1,0:T(1,128)S(1)} %bitcast.17), channel_id=1, source_target_pairs={{0,64},{64,128},{128,192},{192,256},{256,320},{320,384},{384,448},... | collective-permute-start | bytes 18440 | tf_op jit(solution)/shard_map/ppermute | solution.py:26
  27.1 3.6 %collective-permute-start.1 = (f32[3,1,512]{2,1,0:T(1,128)S(1)}, f32[3,1,512]{2,1,0:T(1,128)S(1)}, u32[]{:S(2)}, u32[]{:S(2)}) collective-permute-start(f32[3,1,512]{2,1,0:T(1,128)S(1)} %bitcast.18), channel_id=1, source_target_pairs={{64,0},{128,64},{192,128},{256,192},{320,256},{384,320},{448,384},... | collective-permute-start | bytes 18440 | tf_op jit(solution)/shard_map/ppermute | solution.py:26
  30.8 0.0 collective-permute-done.refs_3_
  30.8 1.3 %collective-permute-done.1.refs_4_ = f32[3,1,512]{2,1,0:T(1,128)S(1)} collective-permute-done((f32[3,1,512]{2,1,0:T(1,128)S(1)}, f32[3,1,512]{2,1,0:T(1,128)S(1)}, u32[]{:S(2)}, u32[]{:S(2)}) %collective-permute-start.1) | collective-permute-done | bytes 6176 | tf_op jit(solution)/shard_map/ppermute | solution.py:26
  32.1 10.4 %all-to-all-done = f32[64,1,1536]{2,1,0:T(1,128)S(1)} async-done(((f32[64,1,1536]{2,1,0:T(1,128)}), f32[64,1,1536]{2,1,0:T(1,128)S(1)}, u32[]{:S(2)}, u32[]{:S(2)}) %all-to-all-start) | async-done | bytes 393248 | tf_op jit(solution)/shard_map/all_to_all | solution.py:308
  42.6 0.0 copy-done
  42.6 0.0 copy-done.1
  42.6 0.1 force.1
  42.7 16.3 %all_to_all.20 = f32[64,1,128]{2,1,0:T(1,128)S(1)} all-to-all(f32[64,1,128]{2,1,0:T(1,128)S(1)} %bitcast.16), channel_id=1, replica_groups=mesh['img'=8,'atom'=64] {'atom'}, dimensions={0} | all-to-all | bytes 65536 | tf_op jit(solution)/shard_map/all_to_all | solution.py:331
  59.0 0.8 %band.1 = (f32[3,1,512]{2,1,0:T(1,128)}, f32[1,128]{1,0:T(1,128)}) custom-call(f32[64,128]{1,0:T(8,128)S(1)} %bitcast.15, f32[12,128]{1,0:T(8,128)S(1)} %get-tuple-element.8.refs_1_, f32[12,128]{1,0:T(8,128)S(1)} %get-tuple-element.9.refs_2_), custom_call_target="tpu_custom_call" | custom-call | flops 8192 | bytes 32768 | tf_op jit(solution)/shard_map/band/pallas_call | solution.py:332
Async XLA Ops:
  1.3 23.9 %copy-start.2 = (f32[1,3,512]{2,0,1:T(1,128)S(1)}, f32[1,3,512]{2,0,1:T(1,128)}, u32[]{:S(2)}) copy-start(f32[1,3,512]{2,0,1:T(1,128)} %param.23) | copy-start | bytes 18436
  1.3 41.3 %copy-start = (f32[3,512]{1,0:T(4,128)S(1)}, f32[3,512]{1,0:T(4,128)}, u32[]{:S(2)}) copy-start(f32[3,512]{1,0:T(4,128)} %refs_5_.3) | copy-start | bytes 18436
  1.3 41.3 %copy-start.1 = (f32[3,512]{1,0:T(4,128)S(1)}, f32[3,512]{1,0:T(4,128)}, u32[]{:S(2)}) copy-start(f32[3,512]{1,0:T(4,128)} %refs_6_.3) | copy-start | bytes 18436
  8.6 34.0 %all-to-all-start = ((f32[64,1,1536]{2,1,0:T(1,128)}), f32[64,1,1536]{2,1,0:T(1,128)S(1)}, u32[]{:S(2)}, u32[]{:S(2)}) async-start(f32[64,1,1536]{2,1,0:T(1,128)} %bitcast.22), calls=%async_computation | async-start | bytes 786432 | tf_op jit(solution)/shard_map/all_to_all | solution.py:308
  25.2 5.6 %collective-permute-start = (f32[3,1,512]{2,1,0:T(1,128)S(1)}, f32[3,1,512]{2,1,0:T(1,128)S(1)}, u32[]{:S(2)}, u32[]{:S(2)}) collective-permute-start(f32[3,1,512]{2,1,0:T(1,128)S(1)} %bitcast.17), channel_id=1, source_target_pairs={{0,64},{64,128},{128,192},{192,256},{256,320},{320,384},{384,448},... | collective-permute-start | bytes 18440 | tf_op jit(solution)/shard_map/ppermute | solution.py:26
  27.1 5.0 %collective-permute-start.1 = (f32[3,1,512]{2,1,0:T(1,128)S(1)}, f32[3,1,512]{2,1,0:T(1,128)S(1)}, u32[]{:S(2)}, u32[]{:S(2)}) collective-permute-start(f32[3,1,512]{2,1,0:T(1,128)S(1)} %bitcast.18), channel_id=1, source_target_pairs={{64,0},{128,64},{192,128},{256,192},{320,256},{384,320},{448,384},... | collective-permute-start | bytes 18440 | tf_op jit(solution)/shard_map/ppermute | solution.py:26

commit v4 on v3

--- a/solution.py
+++ b/solution.py
@@ -144,7 +144,6 @@
             axis=0,
         )
         new = product_nt(row_ref[:, at], spread)
-        new = new[:, : 3 * LANES] + new[:, 3 * LANES :]
         blocks_at = lax.broadcasted_iota(i32, (blocks, CHUNK), 0) == owner_ref[:, at] >> lane_bits
         own_rows = jnp.concatenate(
             [
@@ -174,9 +173,11 @@
     scatter(steps - 1)
     for c in range(3):
         for q in range(blocks):
-            sent_ref[pl.ds(c * blocks + q, owners, stride=3 * blocks), :] = total_ref[
-                q * owners : (q + 1) * owners, c * LANES : (c + 1) * LANES
-            ]
+            from_rows = pl.ds(q * owners, owners)
+            sent_ref[pl.ds(c * blocks + q, owners, stride=3 * blocks), :] = (
+                total_ref[from_rows, c * LANES : (c + 1) * LANES]
+                + total_ref[from_rows, (c + 3) * LANES : (c + 4) * LANES]
+            )
     mine = lax.axis_index("atom") * (3 * blocks)
     for k in range(3 * blocks):
         at = pl.ds(mine + k, 1)
@@ -284,7 +285,7 @@
             vmem((blocks * owners, n_slots), bf16),
             vmem((LANES, n_slots), bf16),
             vmem((LANES, n_slots), bf16),
-            vmem((blocks * owners, 3 * LANES), f32),
+            vmem((blocks * owners, 6 * LANES), f32),
             vmem((2 * rows, LANES), f32),
             vmem((blocks * owners, CHUNK), bf16),
             dma((5,)),

time: 60.1 us -> 59.8 us (level)
  no operation moved by 1% of the time
where the time goes in v4:
time: 59.8 us; the launch traced here: 59.5 us
  starting transfers between devices  22.2 us (37%)
  blocking collectives  16.3 us (27%)
  waiting for transfers between devices  11.8 us (20%)
  Pallas kernels  7.9 us (13%)
  between operations  1.36 us (2%)
    all_to_all x1, starting transfers between devices, local(): lax.all_to_all(sent.reshape(owners, rows * LANES), 'atom', 0, 0, tiled=True)  16.6 us
    all_to_all x1, blocking collectives, local(): parts = lax.all_to_all(parts, 'atom', 0, 0, tiled=True)  16.3 us
    all_to_all x1, waiting for transfers between devices, local(): lax.all_to_all(sent.reshape(owners, rows * LANES), 'atom', 0, 0, tiled=True)  10.4 us
    pallas_call x1, Pallas kernels, local(): pl.pallas_call(lambda *refs: pairs_kernel(blocks, owners, *refs), out_sha...  6.94 us
    ppermute x2, starting transfers between devices, passed_along(): return lax.ppermute(block, axis, route)  5.56 us
    ppermute x2, waiting for transfers between devices, passed_along(): return lax.ppermute(block, axis, route)  1.31 us
  transfers between devices with their start and end apart: 3, of which 2 were waited for; matrix products, arithmetic and copies ran while one was open for 0% of the time, Pallas kernels for 0%

profile of v4, /device:TPU:6, one launch (start us, length us, event | category | flops | bytes accessed | tf_op | source)
XLA Modules:
  0.0 59.5 jit_solution(4009598499050618730)
XLA Ops:
  1.3 0.0 copy-start.2
  1.3 0.0 copy-start
  1.3 0.0 copy-start.1
  1.3 6.9 %pairs.1 = f32[768,128]{1,0:T(8,128)} custom-call(s32[1,1]{1,0:T(1,128)S(6)} %copy.17.refs_0_, s32[4]{0:T(128)} %refs_1_.1, s32[4,128]{1,0:T(4,128)} %bitcast.23, s32[1,3072]{1,0:T(1,128)} %refs_3_.1, s32[1,3072]{1,0:T(1,128)} %refs_4_.1, s32[1,3072]{1,0:T(1,128)} %refs_5_.2, bf16[1,9,9,3072]{3,2,1,0:T(8,128)(2,1)} %refs_6_.2, ...), custom_call_target="tpu_custom_call" | custom-call | flops 1207959552 | bytes 5971968 | tf_op jit(solution)/shard_map/pairs/pallas_call | solution.py:267
  8.3 16.6 %all-to-all-start = ((f32[64,1,1536]{2,1,0:T(1,128)}), f32[64,1,1536]{2,1,0:T(1,128)S(1)}, u32[]{:S(2)}, u32[]{:S(2)}) async-start(f32[64,1,1536]{2,1,0:T(1,128)} %bitcast.22), calls=%async_computation | async-start | bytes 786432 | tf_op jit(solution)/shard_map/all_to_all | solution.py:309
  24.9 0.0 copy-done.2
  24.9 1.9 %collective-permute-start = (f32[3,1,512]{2,1,0:T(1,128)S(1)}, f32[3,1,512]{2,1,0:T(1,128)S(1)}, u32[]{:S(2)}, u32[]{:S(2)}) collective-permute-start(f32[3,1,512]{2,1,0:T(1,128)S(1)} %bitcast.17), channel_id=1, source_target_pairs={{0,64},{64,128},{128,192},{192,256},{256,320},{320,384},{384,448},... | collective-permute-start | bytes 18440 | tf_op jit(solution)/shard_map/ppermute | solution.py:26
  26.8 3.6 %collective-permute-start.1 = (f32[3,1,512]{2,1,0:T(1,128)S(1)}, f32[3,1,512]{2,1,0:T(1,128)S(1)}, u32[]{:S(2)}, u32[]{:S(2)}) collective-permute-start(f32[3,1,512]{2,1,0:T(1,128)S(1)} %bitcast.18), channel_id=1, source_target_pairs={{64,0},{128,64},{192,128},{256,192},{320,256},{384,320},{448,384},... | collective-permute-start | bytes 18440 | tf_op jit(solution)/shard_map/ppermute | solution.py:26
  30.5 0.0 collective-permute-done.refs_3_
  30.5 1.3 %collective-permute-done.1.refs_4_ = f32[3,1,512]{2,1,0:T(1,128)S(1)} collective-permute-done((f32[3,1,512]{2,1,0:T(1,128)S(1)}, f32[3,1,512]{2,1,0:T(1,128)S(1)}, u32[]{:S(2)}, u32[]{:S(2)}) %collective-permute-start.1) | collective-permute-done | bytes 6176 | tf_op jit(solution)/shard_map/ppermute | solution.py:26
  31.8 10.4 %all-to-all-done = f32[64,1,1536]{2,1,0:T(1,128)S(1)} async-done(((f32[64,1,1536]{2,1,0:T(1,128)}), f32[64,1,1536]{2,1,0:T(1,128)S(1)}, u32[]{:S(2)}, u32[]{:S(2)}) %all-to-all-start) | async-done | bytes 393248 | tf_op jit(solution)/shard_map/all_to_all | solution.py:309
  42.2 0.0 copy-done
  42.2 0.0 copy-done.1
  42.2 0.1 force.1
  42.4 16.3 %all_to_all.20 = f32[64,1,128]{2,1,0:T(1,128)S(1)} all-to-all(f32[64,1,128]{2,1,0:T(1,128)S(1)} %bitcast.16), channel_id=1, replica_groups=mesh['img'=8,'atom'=64] {'atom'}, dimensions={0} | all-to-all | bytes 65536 | tf_op jit(solution)/shard_map/all_to_all | solution.py:332
  58.7 0.8 %band.1 = (f32[3,1,512]{2,1,0:T(1,128)}, f32[1,128]{1,0:T(1,128)}) custom-call(f32[64,128]{1,0:T(8,128)S(1)} %bitcast.15, f32[12,128]{1,0:T(8,128)S(1)} %get-tuple-element.8.refs_1_, f32[12,128]{1,0:T(8,128)S(1)} %get-tuple-element.9.refs_2_), custom_call_target="tpu_custom_call" | custom-call | flops 8192 | bytes 32768 | tf_op jit(solution)/shard_map/band/pallas_call | solution.py:333
Async XLA Ops:
  1.3 23.6 %copy-start.2 = (f32[1,3,512]{2,0,1:T(1,128)S(1)}, f32[1,3,512]{2,0,1:T(1,128)}, u32[]{:S(2)}) copy-start(f32[1,3,512]{2,0,1:T(1,128)} %param.23) | copy-start | bytes 18436
  1.3 40.9 %copy-start = (f32[3,512]{1,0:T(4,128)S(1)}, f32[3,512]{1,0:T(4,128)}, u32[]{:S(2)}) copy-start(f32[3,512]{1,0:T(4,128)} %refs_5_.3) | copy-start | bytes 18436
  1.3 40.9 %copy-start.1 = (f32[3,512]{1,0:T(4,128)S(1)}, f32[3,512]{1,0:T(4,128)}, u32[]{:S(2)}) copy-start(f32[3,512]{1,0:T(4,128)} %refs_6_.3) | copy-start | bytes 18436
  8.3 34.0 %all-to-all-start = ((f32[64,1,1536]{2,1,0:T(1,128)}), f32[64,1,1536]{2,1,0:T(1,128)S(1)}, u32[]{:S(2)}, u32[]{:S(2)}) async-start(f32[64,1,1536]{2,1,0:T(1,128)} %bitcast.22), calls=%async_computation | async-start | bytes 786432 | tf_op jit(solution)/shard_map/all_to_all | solution.py:309
  24.9 5.6 %collective-permute-start = (f32[3,1,512]{2,1,0:T(1,128)S(1)}, f32[3,1,512]{2,1,0:T(1,128)S(1)}, u32[]{:S(2)}, u32[]{:S(2)}) collective-permute-start(f32[3,1,512]{2,1,0:T(1,128)S(1)} %bitcast.17), channel_id=1, source_target_pairs={{0,64},{64,128},{128,192},{192,256},{256,320},{320,384},{384,448},... | collective-permute-start | bytes 18440 | tf_op jit(solution)/shard_map/ppermute | solution.py:26
  26.8 5.0 %collective-permute-start.1 = (f32[3,1,512]{2,1,0:T(1,128)S(1)}, f32[3,1,512]{2,1,0:T(1,128)S(1)}, u32[]{:S(2)}, u32[]{:S(2)}) collective-permute-start(f32[3,1,512]{2,1,0:T(1,128)S(1)} %bitcast.18), channel_id=1, source_target_pairs={{64,0},{128,64},{192,128},{256,192},{320,256},{384,320},{448,384},... | collective-permute-start | bytes 18440 | tf_op jit(solution)/shard_map/ppermute | solution.py:26

commit v5 on v4

--- a/solution.py
+++ b/solution.py
@@ -95,7 +95,9 @@
     )
     one, zero = jnp.ones((), bf16), jnp.zeros((), bf16)
     limits = []
-    for step, at in enumerate(spans):
+
+    def prepare(step):
+        at = spans[step]
         owner, partner = owner_ref[:, at], partner_ref[:, at]
         lanes = level_ref[:LANES, :]
         own_at = (owner & (LANES - 1)).astype(f32).astype(bf16)
@@ -161,6 +163,7 @@
             total_ref[...] += new
             own_total_ref[...] += own_new
 
+    prepare(0)
     for step in range(steps):
         for copy in streams[step]:
             copy.wait()
@@ -168,6 +171,8 @@
             for copy in streams[step + DEPTH]:
                 copy.start()
         products(step)
+        if step + 1 < steps:
+            prepare(step + 1)
         if step > 0:
             scatter(step - 1)
     scatter(steps - 1)

time: 59.8 us -> 59.7 us (level)
  no operation moved by 1% of the time
where the time goes in v5:
time: 59.7 us; the launch traced here: 59.4 us
  starting transfers between devices  22.2 us (37%)
  blocking collectives  16.3 us (27%)
  waiting for transfers between devices  11.8 us (20%)
  Pallas kernels  7.76 us (13%)
  between operations  1.36 us (2%)
    all_to_all x1, starting transfers between devices, local(): lax.all_to_all(sent.reshape(owners, rows * LANES), 'atom', 0, 0, tiled=True)  16.6 us
    all_to_all x1, blocking collectives, local(): parts = lax.all_to_all(parts, 'atom', 0, 0, tiled=True)  16.3 us
    all_to_all x1, waiting for transfers between devices, local(): lax.all_to_all(sent.reshape(owners, rows * LANES), 'atom', 0, 0, tiled=True)  10.4 us
    pallas_call x1, Pallas kernels, local(): pl.pallas_call(lambda *refs: pairs_kernel(blocks, owners, *refs), out_sha...  6.8 us
    ppermute x2, starting transfers between devices, passed_along(): return lax.ppermute(block, axis, route)  5.56 us
    ppermute x2, waiting for transfers between devices, passed_along(): return lax.ppermute(block, axis, route)  1.31 us
  transfers between devices with their start and end apart: 3, of which 2 were waited for; matrix products, arithmetic and copies ran while one was open for 0% of the time, Pallas kernels for 0%

profile of v5, /device:TPU:6, one launch (start us, length us, event | category | flops | bytes accessed | tf_op | source)
XLA Modules:
  0.0 59.4 jit_solution(3485911051849357022)
XLA Ops:
  1.3 0.0 copy-start.2
  1.3 0.0 copy-start
  1.3 0.0 copy-start.1
  1.3 6.8 %pairs.1 = f32[768,128]{1,0:T(8,128)} custom-call(s32[1,1]{1,0:T(1,128)S(6)} %copy.17.refs_0_, s32[4]{0:T(128)} %refs_1_.1, s32[4,128]{1,0:T(4,128)} %bitcast.23, s32[1,3072]{1,0:T(1,128)} %refs_3_.1, s32[1,3072]{1,0:T(1,128)} %refs_4_.1, s32[1,3072]{1,0:T(1,128)} %refs_5_.2, bf16[1,9,9,3072]{3,2,1,0:T(8,128)(2,1)} %refs_6_.2, ...), custom_call_target="tpu_custom_call" | custom-call | flops 1207959552 | bytes 5971968 | tf_op jit(solution)/shard_map/pairs/pallas_call | solution.py:272
  8.1 16.6 %all-to-all-start = ((f32[64,1,1536]{2,1,0:T(1,128)}), f32[64,1,1536]{2,1,0:T(1,128)S(1)}, u32[]{:S(2)}, u32[]{:S(2)}) async-start(f32[64,1,1536]{2,1,0:T(1,128)} %bitcast.22), calls=%async_computation | async-start | bytes 786432 | tf_op jit(solution)/shard_map/all_to_all | solution.py:314
  24.7 0.0 copy-done.2
  24.7 1.9 %collective-permute-start = (f32[3,1,512]{2,1,0:T(1,128)S(1)}, f32[3,1,512]{2,1,0:T(1,128)S(1)}, u32[]{:S(2)}, u32[]{:S(2)}) collective-permute-start(f32[3,1,512]{2,1,0:T(1,128)S(1)} %bitcast.17), channel_id=1, source_target_pairs={{0,64},{64,128},{128,192},{192,256},{256,320},{320,384},{384,448},... | collective-permute-start | bytes 18440 | tf_op jit(solution)/shard_map/ppermute | solution.py:26
  26.7 3.6 %collective-permute-start.1 = (f32[3,1,512]{2,1,0:T(1,128)S(1)}, f32[3,1,512]{2,1,0:T(1,128)S(1)}, u32[]{:S(2)}, u32[]{:S(2)}) collective-permute-start(f32[3,1,512]{2,1,0:T(1,128)S(1)} %bitcast.18), channel_id=1, source_target_pairs={{64,0},{128,64},{192,128},{256,192},{320,256},{384,320},{448,384},... | collective-permute-start | bytes 18440 | tf_op jit(solution)/shard_map/ppermute | solution.py:26
  30.3 0.0 collective-permute-done.refs_3_
  30.3 1.3 %collective-permute-done.1.refs_4_ = f32[3,1,512]{2,1,0:T(1,128)S(1)} collective-permute-done((f32[3,1,512]{2,1,0:T(1,128)S(1)}, f32[3,1,512]{2,1,0:T(1,128)S(1)}, u32[]{:S(2)}, u32[]{:S(2)}) %collective-permute-start.1) | collective-permute-done | bytes 6176 | tf_op jit(solution)/shard_map/ppermute | solution.py:26
  31.6 10.4 %all-to-all-done = f32[64,1,1536]{2,1,0:T(1,128)S(1)} async-done(((f32[64,1,1536]{2,1,0:T(1,128)}), f32[64,1,1536]{2,1,0:T(1,128)S(1)}, u32[]{:S(2)}, u32[]{:S(2)}) %all-to-all-start) | async-done | bytes 393248 | tf_op jit(solution)/shard_map/all_to_all | solution.py:314
  42.1 0.0 copy-done
  42.1 0.0 copy-done.1
  42.1 0.1 force.1
  42.2 16.3 %all_to_all.20 = f32[64,1,128]{2,1,0:T(1,128)S(1)} all-to-all(f32[64,1,128]{2,1,0:T(1,128)S(1)} %bitcast.16), channel_id=1, replica_groups=mesh['img'=8,'atom'=64] {'atom'}, dimensions={0} | all-to-all | bytes 65536 | tf_op jit(solution)/shard_map/all_to_all | solution.py:337
  58.5 0.8 %band.1 = (f32[3,1,512]{2,1,0:T(1,128)}, f32[1,128]{1,0:T(1,128)}) custom-call(f32[64,128]{1,0:T(8,128)S(1)} %bitcast.15, f32[12,128]{1,0:T(8,128)S(1)} %get-tuple-element.8.refs_1_, f32[12,128]{1,0:T(8,128)S(1)} %get-tuple-element.9.refs_2_), custom_call_target="tpu_custom_call" | custom-call | flops 8192 | bytes 32768 | tf_op jit(solution)/shard_map/band/pallas_call | solution.py:338
Async XLA Ops:
  1.3 23.4 %copy-start.2 = (f32[1,3,512]{2,0,1:T(1,128)S(1)}, f32[1,3,512]{2,0,1:T(1,128)}, u32[]{:S(2)}) copy-start(f32[1,3,512]{2,0,1:T(1,128)} %param.23) | copy-start | bytes 18436
  1.3 40.8 %copy-start = (f32[3,512]{1,0:T(4,128)S(1)}, f32[3,512]{1,0:T(4,128)}, u32[]{:S(2)}) copy-start(f32[3,512]{1,0:T(4,128)} %refs_5_.3) | copy-start | bytes 18436
  1.3 40.8 %copy-start.1 = (f32[3,512]{1,0:T(4,128)S(1)}, f32[3,512]{1,0:T(4,128)}, u32[]{:S(2)}) copy-start(f32[3,512]{1,0:T(4,128)} %refs_6_.3) | copy-start | bytes 18436
  8.1 34.0 %all-to-all-start = ((f32[64,1,1536]{2,1,0:T(1,128)}), f32[64,1,1536]{2,1,0:T(1,128)S(1)}, u32[]{:S(2)}, u32[]{:S(2)}) async-start(f32[64,1,1536]{2,1,0:T(1,128)} %bitcast.22), calls=%async_computation | async-start | bytes 786432 | tf_op jit(solution)/shard_map/all_to_all | solution.py:314
  24.7 5.6 %collective-permute-start = (f32[3,1,512]{2,1,0:T(1,128)S(1)}, f32[3,1,512]{2,1,0:T(1,128)S(1)}, u32[]{:S(2)}, u32[]{:S(2)}) collective-permute-start(f32[3,1,512]{2,1,0:T(1,128)S(1)} %bitcast.17), channel_id=1, source_target_pairs={{0,64},{64,128},{128,192},{192,256},{256,320},{320,384},{384,448},... | collective-permute-start | bytes 18440 | tf_op jit(solution)/shard_map/ppermute | solution.py:26
  26.7 5.0 %collective-permute-start.1 = (f32[3,1,512]{2,1,0:T(1,128)S(1)}, f32[3,1,512]{2,1,0:T(1,128)S(1)}, u32[]{:S(2)}, u32[]{:S(2)}) collective-permute-start(f32[3,1,512]{2,1,0:T(1,128)S(1)} %bitcast.18), channel_id=1, source_target_pairs={{64,0},{128,64},{192,128},{256,192},{320,256},{384,320},{448,384},... | collective-permute-start | bytes 18440 | tf_op jit(solution)/shard_map/ppermute | solution.py:26
